TPU v7x, 512 devices: a whole 4x8x8 slice. The times are simulated.
512 devices in a mesh: user: 8 (over z), item: 4 (over x), tm: 16 (over y, core).
Axes of the slice: x: 4, y: 8, z: 8, core: 2. Of those that a mesh axis runs over, the one named last changes fastest.
Arguments:
- blocks: bfloat16 [8, 4, 16, 8, 64, 4096], P('user', 'item', 'tm'), may hold values from 0 to 8
- block_coords: int32 [8, 4, 16, 8, 3], P('user', 'item', 'tm'), may hold values from 0 to 127, as said below
- block_count: int32 [8, 4, 16], P('user', 'item', 'tm'), may hold values from 1 to 8, as said below
- a_factor: float32 [8192, 128], P(('user', 'item', 'tm')), as said below
- item_factor: bfloat16 [4096, 128], P(('item', 'user', 'tm')), as said below
- hour_factor: bfloat16 [8192, 128], P(('tm', 'user', 'item')), as said below
Outputs:
- new_factor: float32 [8192, 128], P(('user', 'item', 'tm'))
Inputs may be any that keep to these rules, and one draw needn't show every extreme that they name: `block_coords`: the user block of a slot of device (u, i, t) lies in u * 16 to u * 16 + 15, its item block in i * 16 to i * 16 + 15, its hour block in t * 8 to t * 8 + 7; the 8 slots of a device name distinct blocks; slots at or past the device's count are not part of the tensor. `block_count`: some device lists all 8 slots. `a_factor`: entries are nonnegative. `item_factor`: entries are positive. `hour_factor`: entries are positive.
All inputs are finite; a program needn't handle non-finite values.
Results may differ from a plain program's by a relative error of at most 0.00045.
Values may be sent and summed in bfloat16 or wider, within the bound.
A program may use at most 64 MiB of HBM per device.

v0:
```python
import jax
import jax.numpy as jnp
from jax import lax
from jax.sharding import PartitionSpec as P


def update_column(factor, mttkrp, gram, column):
    weights = lax.dynamic_index_in_dim(gram, column, 1, keepdims=False)
    pivot = lax.dynamic_index_in_dim(weights, column, 0, keepdims=False)
    current = lax.dynamic_index_in_dim(factor, column, 1, keepdims=False)
    target = lax.dynamic_index_in_dim(mttkrp, column, 1, keepdims=False)
    fitted = jnp.dot(factor, weights, precision=lax.Precision.HIGHEST)
    fresh = jnp.maximum(current + (target - fitted) / pivot, 0.0)
    return lax.dynamic_update_index_in_dim(factor, fresh, column, 1)


def self_product(matrix):
    return lax.dot_general(
        matrix, matrix, (((0,), (0,)), ((), ())), preferred_element_type=jnp.float32
    )


def per_device(blocks, block_coords, block_count, a_factor, item_factor, hour_factor):
    tiles = blocks.reshape(blocks.shape[3:])
    coords = block_coords.reshape(block_coords.shape[3:])
    count = block_count.reshape(())
    width = tiles.shape[1]
    rank = item_factor.shape[1]
    item_slab = lax.all_gather(item_factor, ("user", "tm"), axis=0, tiled=True)
    hour_slab = lax.all_gather(hour_factor, ("user", "item"), axis=0, tiled=True)
    hour_blocks = hour_slab.reshape(hour_slab.shape[0] // width, width, rank)
    share_rows = a_factor.shape[0]
    user_rows = share_rows * lax.axis_size("item") * lax.axis_size("tm")
    user_first = lax.axis_index("user") * (user_rows // width)
    item_first = lax.axis_index("item") * (item_slab.shape[0] // width)
    hour_first = lax.axis_index("tm") * hour_blocks.shape[0]

    def add_block(totals, tile, coord, hour_rows):
        item_rows = lax.dynamic_slice_in_dim(
            item_slab, (coord[1] - item_first) * width, width, 0
        ).astype(jnp.float32)
        khatri = (
            (item_rows[:, None, :] * hour_rows.astype(jnp.float32)[None, :, :])
            .reshape(width * width, rank)
            .astype(jnp.bfloat16)
        )
        term = jnp.dot(tile, khatri, preferred_element_type=jnp.float32)
        start = (coord[0] - user_first) * width
        current = lax.dynamic_slice_in_dim(totals, start, width, 0)
        return lax.dynamic_update_slice_in_dim(totals, current + term, start, 0)

    def own_step(slot, totals):
        tile = lax.dynamic_index_in_dim(tiles, slot, 0, keepdims=False)
        coord = lax.dynamic_index_in_dim(coords, slot, 0, keepdims=False)
        hour_rows = lax.dynamic_index_in_dim(hour_blocks, coord[2] - hour_first, 0, keepdims=False)
        return add_block(totals, tile, coord, hour_rows)

    totals = jnp.zeros((user_rows, rank), jnp.float32)
    totals = lax.fori_loop(0, count, own_step, totals)
    summed = lax.psum(totals, ("item", "tm"))
    position = lax.axis_index("item") * lax.axis_size("tm") + lax.axis_index("tm")
    mttkrp = lax.dynamic_slice_in_dim(summed, position * share_rows, share_rows, 0)
    gram_items, gram_hours = lax.psum(
        (self_product(item_factor), self_product(hour_factor)), ("user", "item", "tm")
    )
    gram = gram_items * gram_hours
    group = 16

    def sweep(block, factor):
        for offset in range(group):
            factor = update_column(factor, mttkrp, gram, block * group + offset)
        return factor

    return lax.fori_loop(0, rank // group, sweep, a_factor)


def solution(mesh):
    placed = (
        P("user", "item", "tm", None, None, None),
        P("user", "item", "tm", None, None),
        P("user", "item", "tm"),
        P(("user", "item", "tm"), None),
        P(("item", "user", "tm"), None),
        P(("tm", "user", "item"), None),
    )
    return jax.shard_map(
        per_device,
        mesh=mesh,
        in_specs=placed,
        out_specs=P(("user", "item", "tm"), None),
        check_vma=False,
    )
```

profile of v0, /device:TPU:1, one launch (start us, length us, event | category | flops | bytes accessed | tf_op | source)
XLA Modules:
  0.0 590.0 jit_solution(8561335520772189482)
XLA Ops:
  6.5 1.6 fusion.118
  8.1 1.6 fusion.119
  9.8 58.5 %all_gather.6 = bf16[1024,128]{1,0:T(8,128)(2,1)S(1)} all-gather(bf16[8,128]{1,0:T(8,128)(2,1)} %param.14), channel_id=1, replica_groups=mesh['user'=8,'item'=4,'tm'=16] {'user','tm'}, dimensions={0}, use_global_device_ids=true | all-gather | bytes 264192 | tf_op jit(solution)/shard_map/all_gather | solution.py:29
  68.3 33.2 %all_gather.7 = bf16[512,128]{1,0:T(8,128)(2,1)S(1)} all-gather(bf16[16,128]{1,0:T(8,128)(2,1)} %param.15), channel_id=1, replica_groups=mesh['user'=8,'item'=4,'tm'=16] {'user','item'}, dimensions={0}, use_global_device_ids=true | all-gather | bytes 135168 | tf_op jit(solution)/shard_map/all_gather | solution.py:30
  102.3 15.5 %while.26 = (s32[]{:T(128)}, f32[1024,128]{1,0:T(8,128)S(1)}, s32[]{:T(128)}, s32[8,3]{0,1:T(4,128)S(1)}, s32[]{:T(128)}, /*index=5*/bf16[8,64,4096]{2,1,0:T(8,1...) while((s32[]{:T(128)}, f32[1024,128]{1,0:T(8,128)S(1)}, ...), condition=%wide.region_3.4_spmd, body=%wide.region_2.3_spmd.sunk | while | flops 68182032 | bytes 2851221 | solution.py:59
  105.8 1.4 fusion.181
  110.8 1.4 fusion.181
  115.7 1.4 fusion.181
  117.8 1.0 copy.7
  118.9 161.9 %all-reduce.6.cloned.1.call-done = (f32[128,128]{1,0:T(8,128)}, f32[128,128]{1,0:T(8,128)}) async-done(((f32[128,128]{1,0:T(8,128)}, f32[128,128]{1,0:T(8,128)}), (f32[128,128]{1,0:T(8,128)}, f32[128,128]{1,0:T(8,128)})) %all-reduce.6.cloned.1.call-update) | async-done | bytes 131088 | tf_op jit(solution)/shard_map/psum | solution.py:63
  280.8 0.9 mul.78
  281.8 187.3 %all-reduce.4.cloned.1.call-done = f32[1024,128]{0,1:T(8,128)} async-done(((f32[1024,128]{0,1:T(8,128)}), f32[1024,128]{0,1:T(8,128)}) %all-reduce.4.cloned.1.call-update) | async-done | bytes 524304 | tf_op jit(solution)/shard_map/psum | solution.py:60
  469.1 0.9 constant_dynamic-slice_fusion.65
  470.0 112.5 %while.27 = (s32[]{:T(128)}, f32[16,128]{0,1:T(8,128)S(1)}, f32[16,128]{0,1:T(8,128)S(1)}, f32[128,128]{0,1:T(8,128)S(1)}, s32[]{:T(128)}, /*index=5*/s32[]{:T(1...) while((s32[]{:T(128)}, f32[16,128]{0,1:T(8,128)S(1)}, ...), condition=%wide.region_6.7_spmd, body=%wide.region_5.6_spmd.sunk | while | flops 394322 | bytes 1094245 | solution.py:74
  473.3 0.9 fusion.202
  474.2 0.9 fusion.203
  475.8 0.8 fusion.205
  479.1 0.8 fusion.209
  482.4 0.8 fusion.213
  487.4 0.9 fusion.202
  488.3 0.9 fusion.203
  489.9 0.8 fusion.205
  493.2 0.8 fusion.209
  496.5 0.8 fusion.213
  501.5 0.9 fusion.202
  502.3 0.9 fusion.203
  504.0 0.8 fusion.205
  510.5 0.8 fusion.213
  515.5 0.9 fusion.202
  516.4 0.9 fusion.203
  518.0 0.8 fusion.205
  524.6 0.8 fusion.213
  529.6 0.9 fusion.202
  530.5 0.9 fusion.203
  532.1 0.8 fusion.205
  538.7 0.8 fusion.213
  543.6 0.9 fusion.202
  544.5 0.9 fusion.203
  546.2 0.8 fusion.205
  552.7 0.8 fusion.213
  557.7 0.9 fusion.202
  558.6 0.9 fusion.203
  560.2 0.8 fusion.205
  566.8 0.8 fusion.213
  571.8 0.9 fusion.202
  572.7 0.9 fusion.203
  574.3 0.8 fusion.205
  580.9 0.8 fusion.213
  (256 shorter events, 86.6 us)
Async XLA Ops:
  6.5 274.3 %all-reduce.6.cloned.1.call-start = ((), (), s32[]{:S(2)}) async-start(), calls=%async_computation.1 | async-start | bytes 262144 | tf_op jit(solution)/shard_map/psum | solution.py:63
  9.7 459.4 %all-reduce.4.cloned.1.call-start = ((), (), s32[]{:S(2)}) async-start(), calls=%async_computation | async-start | bytes 1048576 | tf_op jit(solution)/shard_map/psum | solution.py:60
  102.2 16.5 %copy-start = (f32[16,128]{1,0:T(8,128)S(1)}, f32[16,128]{1,0:T(8,128)}, u32[]{:S(2)}) copy-start(f32[16,128]{1,0:T(8,128)} %param.13) | copy-start | bytes 24580
Sparse Core Ops, SparseCore 0:
  12.6 268.2 all-reduce.5
  284.7 184.3 all-reduce.3
where the time goes:
time: 592 us; the launch traced here: 590 us
  waiting for transfers between devices  349 us (59%)
  matrix products  108 us (18%)
  blocking collectives  91.8 us (16%)
  local copies, waits for them, and re-layouts  15.2 us (3%)
  between operations  13.5 us (2%)
  loops' own time  10.4 us (2%)
    psum x1, waiting for transfers between devices, per_device(): summed = lax.psum(totals, ('item', 'tm'))  187 us
    psum x1, waiting for transfers between devices, per_device(): lax.psum((self_product(item_factor), self_product(hour_factor)), ('user',...  162 us
    dot_general x128, matrix products, update_column(): fitted = jnp.dot(factor, weights, precision=lax.Precision.HIGHEST)  101 us
    all_gather x1, blocking collectives, per_device(): item_slab = lax.all_gather(item_factor, ('user', 'tm'), axis=0, tiled=True)  58.5 us
    all_gather x1, blocking collectives, per_device(): lax.all_gather(hour_factor, ('user', 'item'), axis=0, tiled=True)  33.2 us
  transfers between devices with their start and end apart: 2, of which 2 were waited for; matrix products, arithmetic and copies ran while one was open for 2% of the time, Pallas kernels for 0%

commit v1 on v0

v1 whole, which is shorter than its diff:
```python
import functools

import jax
import jax.numpy as jnp
from jax import lax
from jax.experimental import pallas as pl
from jax.experimental.pallas import tpu as pltpu
from jax.sharding import PartitionSpec as P

F32 = jnp.float32
BF16 = jnp.bfloat16
RANK_TILE = 8


def nearest_first(n):
    return sorted(range(1, n), key=lambda d: (min(d, n - d), d))


def farthest_first(n):
    return sorted(range(1, n), key=lambda d: (-min(d, n - d), d))


def self_product(rows):
    return lax.dot_general(rows, rows, (((0,), (0,)), ((), ())), preferred_element_type=F32)


def exchange_kernel(
    nu, ni, nt,
    coords, count, blocks, item, hour,
    mttkrp_out, gram_out,
    items, hours, tiles, terms, totals, from_core, from_x, mine_x, from_y,
    gram_i, gram_h, strip_core, strip_h, strip_y, strip_x, strip, gram,
    tile_sem, z_send, z_recv, zh_send, zh_recv, y_send, y_recv, c_send, c_recv, x_send, x_recv,
    g_send, g_recv, gy_send, gy_recv, gx_send, gx_recv, gz_send, gz_recv,
    rc_send, rc_recv, rx_send, rx_recv, ry_send, ry_recv,
):
    ny = nt // 2
    u = lax.axis_index("user")
    i = lax.axis_index("item")
    t = lax.axis_index("tm")
    y, c = t // 2, t % 2
    slots, width, _ = tiles.shape
    ri, rh = item.shape[0], hour.shape[0]
    rank = item.shape[1]
    share = mttkrp_out.shape[0]
    strip_rows = strip.shape[0]

    def at_user(d):
        return {"user": (u + d) % nu}

    def at_item(d):
        return {"item": (i + d) % ni}

    def at_y(d):
        return {"tm": ((y + d) % ny) * 2 + c}

    sibling = {"tm": y * 2 + 1 - c}

    def remote(src, dst, send, recv, device):
        return pltpu.make_async_remote_copy(
            src_ref=src, dst_ref=dst, send_sem=send, recv_sem=recv,
            device_id=device, device_id_type=pl.DeviceIdType.MESH,
        )

    def tile_copy(s):
        return pltpu.make_async_copy(blocks.at[s], tiles.at[s], tile_sem.at[s])

    for s in range(slots):
        tile_copy(s).start()

    barrier = pltpu.get_barrier_semaphore()
    partners = (
        [at_user(d) for d in range(1, nu)]
        + [at_item(d) for d in range(1, ni)]
        + [at_y(d) for d in range(1, ny)]
        + [sibling]
    )
    for device in partners:
        pl.semaphore_signal(barrier, inc=1, device_id=device, device_id_type=pl.DeviceIdType.MESH)
    items[t, u] = item[...]
    hours[i, u] = hour[...]
    pl.semaphore_wait(barrier, len(partners))

    sent = []

    def start(copy):
        copy.start()
        sent.append(copy)
        return copy

    z_copies = []
    for d in farthest_first(nu):
        z_copies.append(start(remote(hour, hours.at[i, u], zh_send.at[d], zh_recv.at[d], at_user(d))))
        z_copies.append(start(remote(item, items.at[t, u], z_send.at[d], z_recv.at[d], at_user(d))))
    for copy in z_copies:
        copy.wait_recv()

    y_copies = {}
    for d in farthest_first(ny):
        y_copies[d] = start(remote(items.at[t], items.at[t], y_send.at[d], y_recv.at[d], at_y(d)))
    x_copies = []
    for d in farthest_first(ni):
        x_copies.append(start(remote(hours.at[i], hours.at[i], x_send.at[d], x_recv.at[d], at_item(d))))
    c_copies = [start(remote(items.at[t], items.at[t], c_send.at[0], c_recv.at[0], sibling))]
    for d in nearest_first(ny):
        y_copies[d].wait_recv()
        source = ((y + ny - d) % ny) * 2 + c
        c_copies.append(
            start(remote(items.at[source], items.at[source], c_send.at[d], c_recv.at[d], sibling))
        )
    for copy in x_copies:
        copy.wait_recv()

    own_strip = pl.ds(pl.multiple_of(u * strip_rows, strip_rows), strip_rows)
    gram_h[...] = self_product(hours[...].reshape(ni * nu * rh, rank))
    g_copy = start(remote(gram_h.at[own_strip], strip_core, g_send, g_recv, sibling))
    for copy in c_copies:
        copy.wait_recv()
    gram_i[...] = self_product(items[...].reshape(nt * nu * ri, rank))
    gx_copies = [
        start(remote(gram_i.at[own_strip], strip_x.at[d], gx_send.at[d], gx_recv.at[d], at_item(d)))
        for d in farthest_first(ni)
    ]

    user_blocks = (share * ni * nt) // width
    item_blocks = (ri * nu * nt) // width
    hour_blocks = (rh * nu * ni) // width
    span = width // ri
    per_user = nt // span

    def products(low, high):
        @pl.loop(low, high)
        def _(s):
            tile_copy(s).wait()
            item_block = lax.rem(coords[s, 1], item_blocks)
            hour_block = lax.rem(coords[s, 2], hour_blocks)
            item_rows = (
                items[pl.ds(lax.rem(item_block, per_user) * span, span), lax.div(item_block, per_user)]
                .astype(F32)
                .reshape(width, rank)
            )
            hour_rows = hours[:, hour_block].astype(F32).reshape(width, rank)
            group = 16
            term = jnp.zeros((width, rank), F32)
            for g in range(width // group):
                khatri = jnp.concatenate(
                    [
                        (item_rows[j : j + 1, :] * hour_rows).astype(BF16)
                        for j in range(g * group, (g + 1) * group)
                    ],
                    axis=0,
                )
                part = tiles[s, :, g * group * width : (g + 1) * group * width]
                term = term + jnp.dot(part, khatri, preferred_element_type=F32)
            terms[s] = term

    cuts = [slots * k // 4 for k in range(5)]
    products(cuts[0], cuts[1])

    g_copy.wait_recv()
    strip_h[...] = gram_h[own_strip, :] + strip_core[...]
    gy_copies = [
        start(remote(strip_h, strip_y.at[d], gy_send.at[d], gy_recv.at[d], at_y(d)))
        for d in farthest_first(ny)
    ]
    products(cuts[1], cuts[2])

    for copy in gy_copies + gx_copies:
        copy.wait_recv()
    sum_h = strip_h[...]
    for d in range(1, ny):
        sum_h = sum_h + strip_y[d]
    sum_i = gram_i[own_strip, :]
    for d in range(1, ni):
        sum_i = sum_i + strip_x[d]
    strip[...] = sum_h * sum_i
    gram[own_strip, :] = strip[...]
    gz_copies = [
        start(remote(strip, gram.at[own_strip], gz_send.at[d], gz_recv.at[d], at_user(d)))
        for d in farthest_first(nu)
    ]
    products(cuts[2], cuts[4])

    chunks = width // share

    @pl.loop(0, user_blocks)
    def _(b):
        total = jnp.zeros((width, rank), F32)
        for s in range(slots):
            block = jnp.where(s < count[0], lax.rem(coords[s, 0], user_blocks), -1)
            hit = jnp.full((width, rank), block, jnp.int32) == b
            total = total + jnp.where(hit, terms[s], 0.0)
        for q in range(chunks):
            totals[q % 2, b * (chunks // 2) + q // 2] = total[q * share : (q + 1) * share]

    order = farthest_first(ni) + [0]

    def group_of(d):
        return pl.ds(((i + d) % ni) * ny, ny)

    rc_copies = {}
    for d in order:
        rc_copies[d] = start(
            remote(totals.at[1 - c, group_of(d)], from_core.at[group_of(d)], rc_send.at[d], rc_recv.at[d], sibling)
        )
    rx_copies = []
    for d in order:
        rc_copies[d].wait_recv()
        totals[c, group_of(d)] = totals[c, group_of(d)] + from_core[group_of(d)]
        if d:
            rx_copies.append(
                start(remote(totals.at[c, group_of(d)], from_x.at[d], rx_send.at[d], rx_recv.at[d], at_item(d)))
            )
    summed = totals[c, group_of(0)]
    for copy in rx_copies:
        copy.wait_recv()
    for d in range(1, ni):
        summed = summed + from_x[d]
    mine_x[...] = summed
    ry_copies = [
        start(remote(mine_x.at[(y + d) % ny], from_y.at[d], ry_send.at[d], ry_recv.at[d], at_y(d)))
        for d in farthest_first(ny)
    ]
    for copy in gz_copies:
        copy.wait_recv()
    gram_out[...] = gram[...]
    result = mine_x[y]
    for copy in ry_copies:
        copy.wait_recv()
    for d in range(1, ny):
        result = result + from_y[d]
    mttkrp_out[...] = result
    for copy in sent:
        copy.wait_send()


def sweep_kernel(mttkrp, gram, factor, out):
    share, rank = factor.shape
    lanes = 128
    pieces = rank // RANK_TILE
    weights = gram[...]
    current = factor[...]
    fitted = jnp.dot(current, weights, precision=lax.Precision.HIGHEST, preferred_element_type=F32)
    residual = mttkrp[...] - fitted

    def columns_first(x):
        return jnp.concatenate([x] * (lanes // share), axis=0).T

    rows = lax.broadcasted_iota(jnp.int32, (rank, rank), 0)
    cols = lax.broadcasted_iota(jnp.int32, (rank, rank), 1)
    pivot = jnp.sum(jnp.where(rows == cols, weights, 0.0), axis=1, keepdims=True)
    pivot = jnp.broadcast_to(pivot, (rank, lanes))
    scaled = weights / pivot
    start = columns_first(current)
    level = start + columns_first(residual) / pivot

    def split(x):
        return [x[g * RANK_TILE : (g + 1) * RANK_TILE] for g in range(pieces)]

    level, start, scaled = split(level), split(start), split(scaled)
    place = lax.broadcasted_iota(jnp.int32, (RANK_TILE, lanes), 0)
    fresh = []
    for g in range(pieces):
        done = jnp.zeros((RANK_TILE, lanes), F32)
        for k in range(RANK_TILE):
            r = g * RANK_TILE + k
            new = jnp.maximum(level[g], 0.0)
            change = (new - start[g])[k : k + 1, :]
            change = jnp.broadcast_to(change, (RANK_TILE, lanes))
            done = jnp.where(place == k, new, done)
            for h in range(g, pieces):
                weight = jnp.broadcast_to(scaled[h][:, r : r + 1], (RANK_TILE, lanes))
                level[h] = level[h] - weight * change
        fresh.append(done)
    out[...] = jnp.concatenate(fresh, axis=0).T[:share]


def per_device(nu, ni, nt, blocks, block_coords, block_count, a_factor, item_factor, hour_factor):
    tiles = blocks.reshape(blocks.shape[3:])
    coords = block_coords.reshape(block_coords.shape[3:])
    count = block_count.reshape((1,))
    slots, width, depth = tiles.shape
    share, rank = a_factor.shape
    ri, rh = item_factor.shape[0], hour_factor.shape[0]
    ny = nt // 2
    strip_rows = rank // nu
    vmem = pl.BlockSpec(memory_space=pltpu.VMEM)
    smem = pl.BlockSpec(memory_space=pltpu.SMEM)
    dma = pltpu.SemaphoreType.DMA
    mttkrp, gram = pl.pallas_call(
        functools.partial(exchange_kernel, nu, ni, nt),
        out_shape=(
            jax.ShapeDtypeStruct((share, rank), F32),
            jax.ShapeDtypeStruct((rank, rank), F32),
        ),
        in_specs=[smem, smem, pl.BlockSpec(memory_space=pltpu.MemorySpace.HBM), vmem, vmem],
        out_specs=(vmem, vmem),
        scratch_shapes=[
            pltpu.VMEM((nt, nu, ri, rank), BF16),
            pltpu.VMEM((ni, nu, rh, rank), BF16),
            pltpu.VMEM((slots, width, depth), BF16),
            pltpu.VMEM((slots, width, rank), F32),
            pltpu.VMEM((2, ni * ny, share, rank), F32),
            pltpu.VMEM((ni * ny, share, rank), F32),
            pltpu.VMEM((ni, ny, share, rank), F32),
            pltpu.VMEM((ny, share, rank), F32),
            pltpu.VMEM((ny, share, rank), F32),
            pltpu.VMEM((rank, rank), F32),
            pltpu.VMEM((rank, rank), F32),
            pltpu.VMEM((strip_rows, rank), F32),
            pltpu.VMEM((strip_rows, rank), F32),
            pltpu.VMEM((ny, strip_rows, rank), F32),
            pltpu.VMEM((ni, strip_rows, rank), F32),
            pltpu.VMEM((strip_rows, rank), F32),
            pltpu.VMEM((rank, rank), F32),
            dma((slots,)),
            dma((nu,)), dma((nu,)), dma((nu,)), dma((nu,)),
            dma((ny,)), dma((ny,)), dma((ny,)), dma((ny,)), dma((ni,)), dma((ni,)),
            dma, dma, dma((ny,)), dma((ny,)), dma((ni,)), dma((ni,)), dma((nu,)), dma((nu,)),
            dma((ni,)), dma((ni,)), dma((ni,)), dma((ni,)), dma((ny,)), dma((ny,)),
        ],
        compiler_params=pltpu.CompilerParams(
            collective_id=0, has_side_effects=True, vmem_limit_bytes=58 * 1024 * 1024
        ),
        name="exchange",
    )(coords, count, tiles, item_factor, hour_factor)
    return pl.pallas_call(
        sweep_kernel,
        out_shape=jax.ShapeDtypeStruct((share, rank), F32),
        in_specs=[vmem, vmem, vmem],
        out_specs=vmem,
        compiler_params=pltpu.CompilerParams(vmem_limit_bytes=8 * 1024 * 1024),
        name="sweep",
    )(mttkrp, gram, a_factor)


def solution(mesh):
    placed = (
        P("user", "item", "tm", None, None, None),
        P("user", "item", "tm", None, None),
        P("user", "item", "tm"),
        P(("user", "item", "tm"), None),
        P(("item", "user", "tm"), None),
        P(("tm", "user", "item"), None),
    )
    return jax.shard_map(
        functools.partial(per_device, mesh.shape["user"], mesh.shape["item"], mesh.shape["tm"]),
        mesh=mesh,
        in_specs=placed,
        out_specs=P(("user", "item", "tm"), None),
        check_vma=False,
    )
```

time: 592 us -> 51.8 us (0.09)
  waiting for transfers between devices: 349 us -> 0 us
  matrix products: 108 us -> 0 us
  blocking collectives: 91.8 us -> 0 us
  Pallas kernels: 0 us -> 47.9 us
  between operations: 13.5 us -> 0.69 us
  local copies, waits for them, and re-layouts: 15.2 us -> 2.88 us
  loops' own time: 10.4 us -> 0 us
    psum x2 -> x0, waiting for transfers between devices: 349 us -> none  [the longest x1 187 us: per_device(): summed = lax.psum(totals, ('item', 'tm'))]
    dot_general x133 -> x0, matrix products: 108 us -> none  [the longest x128 101 us: update_column(): fitted = jnp.dot(factor, weights, precision=lax.Precision.HIGHEST)]
    all_gather x2 -> x0, blocking collectives: 91.8 us -> none  [the longest x1 58.5 us: per_device(): item_slab = lax.all_gather(item_factor, ('user', 'tm'), axis=0, tiled=True)]
    pallas_call x0 -> x2, Pallas kernels: none -> 47.9 us  [the longest x1 45.6 us: per_device(): pl.pallas_call(functools.partial(exchange_kernel, nu, ni, nt), out_shape=...]
    another operation x2 -> x0, loops' own time: 10.4 us -> none  [the longest x1 8.49 us: per_device(): totals = lax.fori_loop(0, count, own_step, totals)]
    dynamic_slice x12 -> x0, local copies, waits for them, and re-layouts: 7.33 us -> none  [the longest x8 6.19 us: update_column(): pivot = lax.dynamic_index_in_dim(weights, column, 0, keepdims=False)]
  transfers between devices with their start and end apart: 2 -> 0, of which waited for: 2 -> 0; matrix products, arithmetic and copies ran while one was open for 2% -> 0% of each run, Pallas kernels for 0% -> 0%
where the time goes in v1:
time: 51.8 us; the launch traced here: 51.5 us
  Pallas kernels  47.9 us (92%)
  local copies, waits for them, and re-layouts  2.88 us (6%)
  between operations  0.69 us (1%)
    pallas_call x1, Pallas kernels, per_device(): pl.pallas_call(functools.partial(exchange_kernel, nu, ni, nt), out_shape=...  45.6 us
    pallas_call x1, Pallas kernels, per_device(): pl.pallas_call(sweep_kernel, out_shape=jax.ShapeDtypeStruct((share, rank)...  2.3 us
    unnamed x6, local copies, waits for them, and re-layouts  1.53 us
    reshape x1, local copies, waits for them, and re-layouts, per_device(): coords = block_coords.reshape(block_coords.shape[3:])  1.35 us

profile of v1, /device:TPU:1, one launch (start us, length us, event | category | flops | bytes accessed | tf_op | source)
XLA Modules:
  0.0 51.5 jit_solution(2777841181858228764)
XLA Ops:
  0.0 0.0 copy-start.1
  0.7 1.3 %copy.8 = s32[1,1,1,8,3]{4,3,2,1,0:T(8,128)} copy(s32[1,1,1,8,3]{3,2,4,1,0:T(1,128)} %param.7) | data formatting | bytes 192 | tf_op jit(solution)/shard_map/reshape | solution.py:280
  2.0 45.6 %exchange.1 = (f32[16,128]{1,0:T(8,128)}, f32[128,128]{1,0:T(8,128)}) custom-call(s32[8,3]{1,0:T(8,128)} %bitcast.5, s32[1]{0:T(128)} %bitcast.3.count, bf16[8,64,4096]{2,1,0:T(8,128)(2,1)} %bitcast.4, bf16[8,128]{1,0:T(8,128)(2,1)} %item.1, bf16[16,128]{1,0:T(8,128)(2,1)} %hour.1), custom_call_target="tpu_custom_call" | custom-call | tf_op jit(solution)/shard_map/exchange/pallas_call | solution.py:290
  47.7 0.0 copy-done.1
  47.7 0.0 copy-start
  47.7 0.8 %copy-done = f32[128,128]{1,0:T(8,128)S(1)} copy-done((f32[128,128]{1,0:T(8,128)S(1)}, f32[128,128]{1,0:T(8,128)}, u32[]{:S(2)}) %copy-start) | copy-done | bytes 65560
  48.5 0.0 copy-start.2
  48.5 0.7 %copy-done.2 = f32[16,128]{1,0:T(8,128)S(1)} copy-done((f32[16,128]{1,0:T(8,128)S(1)}, f32[16,128]{1,0:T(8,128)}, u32[]{:S(2)}) %copy-start.2) | copy-done | bytes 8216
  49.2 2.3 %sweep.1 = f32[16,128]{1,0:T(8,128)} custom-call(f32[16,128]{1,0:T(8,128)S(1)} %copy-done.2, f32[128,128]{1,0:T(8,128)S(1)} %copy-done, f32[16,128]{1,0:T(8,128)S(1)} %copy-done.1), custom_call_target="tpu_custom_call" | custom-call | tf_op jit(solution)/shard_map/sweep/pallas_call | solution.py:327
Async XLA Ops:
  0.0 47.7 %copy-start.1 = (f32[16,128]{1,0:T(8,128)S(1)}, f32[16,128]{1,0:T(8,128)}, u32[]{:S(2)}) copy-start(f32[16,128]{1,0:T(8,128)} %factor.1) | copy-start | bytes 24580
  47.7 0.8 %copy-start = (f32[128,128]{1,0:T(8,128)S(1)}, f32[128,128]{1,0:T(8,128)}, u32[]{:S(2)}) copy-start(f32[128,128]{1,0:T(8,128)} %get-tuple-element.8.gram) | copy-start | bytes 196612
  48.5 0.7 %copy-start.2 = (f32[16,128]{1,0:T(8,128)S(1)}, f32[16,128]{1,0:T(8,128)}, u32[]{:S(2)}) copy-start(f32[16,128]{1,0:T(8,128)} %get-tuple-element.7.mttkrp) | copy-start | bytes 24580

commit v2 on v1

v2 whole, which is shorter than its diff:
```python
import functools

import jax
import jax.numpy as jnp
from jax import lax
from jax.experimental import pallas as pl
from jax.experimental.pallas import tpu as pltpu
from jax.sharding import PartitionSpec as P

F32 = jnp.float32
BF16 = jnp.bfloat16
ROWS = 8
LANES = 128


def nearest_first(n):
    return sorted(range(1, n), key=lambda d: (min(d, n - d), d))


def farthest_first(n):
    return sorted(range(1, n), key=lambda d: (-min(d, n - d), d))


def self_product(rows):
    return lax.dot_general(rows, rows, (((0,), (0,)), ((), ())), preferred_element_type=F32)


def split(x, rows):
    return [x[k * rows : (k + 1) * rows] for k in range(x.shape[0] // rows)]


def columns_first(x):
    return jnp.concatenate([x] * (LANES // x.shape[0]), axis=0).T


def exchange_kernel(
    nu, ni, nt,
    coords_hbm, count_hbm, blocks, factor_hbm, item_hbm, hour_hbm,
    out,
    coords, count, factor, items, hours, tiles, terms, totals, from_core, from_x, mine_x, from_y,
    grams, g_core, g_mine, g_x, g_sum, g_y, gram,
    in_sem, tile_sem, z_send, z_recv, zh_send, zh_recv, y_send, y_recv, c_send, c_recv, x_send, x_recv,
    gc_send, gc_recv, gx_send, gx_recv, gy_send, gy_recv, gz_send, gz_recv,
    rc_send, rc_recv, rx_send, rx_recv, ry_send, ry_recv,
):
    ny = nt // 2
    u = lax.axis_index("user")
    i = lax.axis_index("item")
    t = lax.axis_index("tm")
    y, c = t // 2, t % 2
    slots, width, _ = tiles.shape
    ri, rh = item_hbm.shape[0], hour_hbm.shape[0]
    share, rank = factor.shape
    strip_rows = rank // nu

    def at_user(d):
        return {"user": (u + d) % nu}

    def at_item(d):
        return {"item": (i + d) % ni}

    def at_y(d):
        return {"tm": ((y + d) % ny) * 2 + c}

    sibling = {"tm": y * 2 + 1 - c}

    def remote(src, dst, send, recv, device):
        return pltpu.make_async_remote_copy(
            src_ref=src, dst_ref=dst, send_sem=send, recv_sem=recv,
            device_id=device, device_id_type=pl.DeviceIdType.MESH,
        )

    def tile_copy(s):
        return pltpu.make_async_copy(blocks.at[s], tiles.at[s], tile_sem.at[s])

    own_rows = [
        pltpu.make_async_copy(hour_hbm, hours.at[i, u], in_sem.at[0]),
        pltpu.make_async_copy(item_hbm, items.at[t, u], in_sem.at[1]),
    ]
    later = [
        pltpu.make_async_copy(factor_hbm, factor, in_sem.at[2]),
        pltpu.make_async_copy(coords_hbm, coords, in_sem.at[3]),
        pltpu.make_async_copy(count_hbm, count, in_sem.at[4]),
    ]
    for copy in own_rows:
        copy.start()

    barrier = pltpu.get_barrier_semaphore()
    partners = (
        [at_user(d) for d in farthest_first(nu)]
        + [at_item(d) for d in farthest_first(ni)]
        + [at_y(d) for d in farthest_first(ny)]
        + [sibling]
    )
    for device in partners:
        pl.semaphore_signal(barrier, inc=1, device_id=device, device_id_type=pl.DeviceIdType.MESH)
    for copy in own_rows:
        copy.wait()
    pl.semaphore_wait(barrier, len(partners))

    sent = []

    def start(copy):
        copy.start()
        sent.append(copy)
        return copy

    z_copies = []
    for d in farthest_first(nu):
        z_copies.append(start(remote(hours.at[i, u], hours.at[i, u], zh_send.at[d], zh_recv.at[d], at_user(d))))
        z_copies.append(start(remote(items.at[t, u], items.at[t, u], z_send.at[d], z_recv.at[d], at_user(d))))
    for copy in later:
        copy.start()
    for s in range(slots):
        tile_copy(s).start()
    for copy in z_copies:
        copy.wait_recv()

    y_copies = {}
    for d in farthest_first(ny):
        y_copies[d] = start(remote(items.at[t], items.at[t], y_send.at[d], y_recv.at[d], at_y(d)))
    x_copies = []
    for d in farthest_first(ni):
        x_copies.append(start(remote(hours.at[i], hours.at[i], x_send.at[d], x_recv.at[d], at_item(d))))
    c_copies = [start(remote(items.at[t], items.at[t], c_send.at[0], c_recv.at[0], sibling))]

    own_strip = pl.ds(pl.multiple_of(u * strip_rows, strip_rows), strip_rows)
    grams[0] = self_product(hours[i].reshape(nu * rh, rank))
    grams[1] = self_product(items[t].reshape(nu * ri, rank))
    gc_copy = start(remote(grams.at[:, own_strip], g_core, gc_send, gc_recv, sibling))
    gc_copy.wait_recv()
    g_mine[...] = grams[:, own_strip] + g_core[...]
    gx_copies = [
        start(remote(g_mine, g_x.at[d], gx_send.at[d], gx_recv.at[d], at_item(d)))
        for d in farthest_first(ni)
    ]

    for d in nearest_first(ny):
        y_copies[d].wait_recv()
        source = ((y + ny - d) % ny) * 2 + c
        c_copies.append(
            start(remote(items.at[source], items.at[source], c_send.at[d], c_recv.at[d], sibling))
        )
    for copy in gx_copies:
        copy.wait_recv()
    g_total = g_mine[...]
    for d in range(1, ni):
        g_total = g_total + g_x[d]
    g_sum[...] = g_total
    gy_copies = [
        start(remote(g_sum, g_y.at[d], gy_send.at[d], gy_recv.at[d], at_y(d)))
        for d in farthest_first(ny)
    ]
    for copy in later:
        copy.wait()
    for copy in x_copies:
        copy.wait_recv()
    for copy in c_copies:
        copy.wait_recv()

    user_blocks = (share * ni * nt) // width
    item_blocks = (ri * nu * nt) // width
    hour_blocks = (rh * nu * ni) // width
    span = width // ri
    per_user = nt // span
    group = 16

    @pl.loop(0, slots)
    def _(s):
        tile_copy(s).wait()
        item_block = lax.rem(coords[1, 0, s], item_blocks)
        hour_block = lax.rem(coords[2, 0, s], hour_blocks)
        item_rows = (
            items[pl.ds(lax.rem(item_block, per_user) * span, span), lax.div(item_block, per_user)]
            .astype(F32)
            .reshape(width, rank)
        )
        hour_rows = hours[:, hour_block].astype(F32).reshape(width, rank)
        term = jnp.zeros((width, rank), F32)
        for g in range(width // group):
            khatri = jnp.concatenate(
                [(item_rows[j : j + 1, :] * hour_rows).astype(BF16) for j in range(g * group, (g + 1) * group)],
                axis=0,
            )
            part = tiles[s, :, g * group * width : (g + 1) * group * width]
            term = term + jnp.dot(part, khatri, preferred_element_type=F32)
        terms[s] = term

    chunks = width // share

    @pl.loop(0, user_blocks)
    def _(b):
        total = jnp.zeros((width, rank), F32)
        for s in range(slots):
            block = jnp.where(s < count[0, 0, 0], lax.rem(coords[0, 0, s], user_blocks), -1)
            hit = jnp.full((width, rank), block, jnp.int32) == b
            total = total + jnp.where(hit, terms[s], 0.0)
        for q in range(chunks):
            totals[q % 2, b * (chunks // 2) + q // 2] = total[q * share : (q + 1) * share]

    order = farthest_first(ni) + [0]

    def group_of(d):
        return pl.ds(((i + d) % ni) * ny, ny)

    rc_copies = {}
    for d in order:
        rc_copies[d] = start(
            remote(totals.at[1 - c, group_of(d)], from_core.at[group_of(d)], rc_send.at[d], rc_recv.at[d], sibling)
        )
    rx_copies = []
    for d in order:
        rc_copies[d].wait_recv()
        totals[c, group_of(d)] = totals[c, group_of(d)] + from_core[group_of(d)]
        if d:
            rx_copies.append(
                start(remote(totals.at[c, group_of(d)], from_x.at[d], rx_send.at[d], rx_recv.at[d], at_item(d)))
            )

    for copy in gy_copies:
        copy.wait_recv()
    g_total = g_sum[...]
    for d in range(1, ny):
        g_total = g_total + g_y[d]
    gram[own_strip, :] = g_total[0] * g_total[1]
    gz_copies = [
        start(remote(gram.at[own_strip], gram.at[own_strip], gz_send.at[d], gz_recv.at[d], at_user(d)))
        for d in farthest_first(nu)
    ]

    summed = totals[c, group_of(0)]
    for copy in rx_copies:
        copy.wait_recv()
    for d in range(1, ni):
        summed = summed + from_x[d]
    mine_x[...] = summed
    ry_copies = [
        start(remote(mine_x.at[(y + d) % ny], from_y.at[d], ry_send.at[d], ry_recv.at[d], at_y(d)))
        for d in farthest_first(ny)
    ]

    for copy in gz_copies:
        copy.wait_recv()
    weights = gram[...]
    current = factor[...]
    fitted = jnp.dot(current, weights, precision=lax.Precision.HIGHEST, preferred_element_type=F32)
    rows = lax.broadcasted_iota(jnp.int32, (rank, rank), 0)
    cols = lax.broadcasted_iota(jnp.int32, (rank, rank), 1)
    pivot = jnp.sum(jnp.where(rows == cols, weights, 0.0), axis=1, keepdims=True)
    pivot = jnp.broadcast_to(pivot, (rank, LANES))
    scaled = weights / pivot
    before = columns_first(current)

    for copy in ry_copies:
        copy.wait_recv()
    mttkrp = mine_x[y]
    for d in range(1, ny):
        mttkrp = mttkrp + from_y[d]

    level = before + columns_first(mttkrp - fitted) / pivot
    place = lax.broadcasted_iota(jnp.int32, (ROWS, LANES), 0)
    fresh = []
    for g in range(rank // ROWS):
        low, high = g * ROWS, (g + 1) * ROWS
        head, rest = level[:ROWS], level[ROWS:]
        old = before[low:high]
        done = head
        for k in range(ROWS):
            new = jnp.maximum(head, 0.0)
            change = jnp.broadcast_to((new - old)[k : k + 1], (ROWS, LANES))
            done = jnp.where(place == k, new, done)
            if k < ROWS - 1:
                head = head - jnp.broadcast_to(scaled[low:high, low + k : low + k + 1], (ROWS, LANES)) * change
            if rest.shape[0]:
                full = jnp.concatenate([change] * (rest.shape[0] // ROWS), axis=0)
                rest = rest - jnp.broadcast_to(scaled[high:, low + k : low + k + 1], rest.shape) * full
        fresh.append(done)
        level = rest
    out[...] = jnp.concatenate(fresh, axis=0).T[:share]
    for copy in sent:
        copy.wait_send()


def per_device(nu, ni, nt, blocks, block_coords, block_count, a_factor, item_factor, hour_factor):
    tiles = blocks.reshape(blocks.shape[3:])
    slots, width, depth = tiles.shape
    coords = jnp.transpose(block_coords, (0, 1, 4, 2, 3)).reshape(3, 1, slots)
    count = block_count.reshape((1, 1, 1))
    share, rank = a_factor.shape
    ri, rh = item_factor.shape[0], hour_factor.shape[0]
    ny = nt // 2
    strip_rows = rank // nu
    hbm = pl.BlockSpec(memory_space=pltpu.MemorySpace.HBM)
    vmem, smem, dma = pltpu.VMEM, pltpu.SMEM, pltpu.SemaphoreType.DMA
    return pl.pallas_call(
        functools.partial(exchange_kernel, nu, ni, nt),
        out_shape=jax.ShapeDtypeStruct((share, rank), F32),
        in_specs=[hbm] * 6,
        out_specs=pl.BlockSpec(memory_space=pltpu.VMEM),
        scratch_shapes=[
            smem((3, 1, slots), jnp.int32),
            smem((1, 1, 1), jnp.int32),
            vmem((share, rank), F32),
            vmem((nt, nu, ri, rank), BF16),
            vmem((ni, nu, rh, rank), BF16),
            vmem((slots, width, depth), BF16),
            vmem((slots, width, rank), F32),
            vmem((2, ni * ny, share, rank), F32),
            vmem((ni * ny, share, rank), F32),
            vmem((ni, ny, share, rank), F32),
            vmem((ny, share, rank), F32),
            vmem((ny, share, rank), F32),
            vmem((2, rank, rank), F32),
            vmem((2, strip_rows, rank), F32),
            vmem((2, strip_rows, rank), F32),
            vmem((ni, 2, strip_rows, rank), F32),
            vmem((2, strip_rows, rank), F32),
            vmem((ny, 2, strip_rows, rank), F32),
            vmem((rank, rank), F32),
            dma((5,)),
            dma((slots,)),
            dma((nu,)), dma((nu,)), dma((nu,)), dma((nu,)),
            dma((ny,)), dma((ny,)), dma((ny,)), dma((ny,)), dma((ni,)), dma((ni,)),
            dma, dma, dma((ni,)), dma((ni,)), dma((ny,)), dma((ny,)), dma((nu,)), dma((nu,)),
            dma((ni,)), dma((ni,)), dma((ni,)), dma((ni,)), dma((ny,)), dma((ny,)),
        ],
        compiler_params=pltpu.CompilerParams(
            collective_id=0, has_side_effects=True, vmem_limit_bytes=58 * 1024 * 1024
        ),
        name="exchange",
    )(coords, count, tiles, a_factor, item_factor, hour_factor)


def solution(mesh):
    placed = (
        P("user", "item", "tm", None, None, None),
        P("user", "item", "tm", None, None),
        P("user", "item", "tm"),
        P(("user", "item", "tm"), None),
        P(("item", "user", "tm"), None),
        P(("tm", "user", "item"), None),
    )
    return jax.shard_map(
        functools.partial(per_device, mesh.shape["user"], mesh.shape["item"], mesh.shape["tm"]),
        mesh=mesh,
        in_specs=placed,
        out_specs=P(("user", "item", "tm"), None),
        check_vma=False,
    )
```

time: 51.8 us -> 43.3 us (0.84); the launches traced: 51.5 us -> 42.4 us
  Pallas kernels: 47.9 us -> 40.5 us
  local copies, waits for them, and re-layouts: 2.88 us -> 1.3 us
    pallas_call x1, Pallas kernels: 45.6 us -> 40.5 us  [per_device(): pl.pallas_call(functools.partial(exchange_kernel, nu, ni, nt), out_shape=...]
    pallas_call x1 -> x0, Pallas kernels: 2.3 us -> none  [per_device(): pl.pallas_call(sweep_kernel, out_shape=jax.ShapeDtypeStruct((share, rank)...]
    reshape x1 -> x0, local copies, waits for them, and re-layouts: 1.35 us -> none  [per_device(): coords = block_coords.reshape(block_coords.shape[3:])]
    unnamed x6 -> x1, local copies, waits for them, and re-layouts: 1.53 us -> 1.3 us
where the time goes in v2:
time: 43.3 us; the launch traced here: 42.4 us
  Pallas kernels  40.5 us (94%)
  local copies, waits for them, and re-layouts  1.3 us (3%)
  between operations  0.66 us (2%)
    pallas_call x1, Pallas kernels, per_device(): pl.pallas_call(functools.partial(exchange_kernel, nu, ni, nt), out_shape=...  40.5 us
    unnamed x1, local copies, waits for them, and re-layouts  1.3 us

profile of v2, /device:TPU:1, one launch (start us, length us, event | category | flops | bytes accessed | tf_op | source)
XLA Modules:
  0.0 42.4 jit_solution(1264953912130938310)
XLA Ops:
  0.7 40.5 %exchange.1 = f32[16,128]{1,0:T(8,128)} custom-call(s32[3,1,8]{2,1,0:T(1,128)} %bitcast.5, s32[1,1,1]{2,1,0:T(1,128)S(6)} %copy.8.count_hbm, bf16[8,64,4096]{2,1,0:T(8,128)(2,1)} %bitcast.4, f32[16,128]{1,0:T(8,128)} %factor_hbm.1, bf16[8,128]{1,0:T(8,128)(2,1)} %item_hbm.1, bf16[16,128]{1,0:T(8,128)(2,1)} %hour_hbm.1), custom_call_target="tpu_custom_call" | custom-call | tf_op jit(solution)/shard_map/exchange/pallas_call | solution.py:295
  41.1 1.3 %copy.9 = f32[16,128]{1,0:T(8,128)} copy(f32[16,128]{1,0:T(8,128)} %exchange.1) | data formatting | bytes 16384

commit v3 on v2

v3 whole, which is shorter than its diff:
```python
import functools

import jax
import jax.numpy as jnp
from jax import lax
from jax.experimental import pallas as pl
from jax.experimental.pallas import tpu as pltpu
from jax.sharding import PartitionSpec as P

F32 = jnp.float32
BF16 = jnp.bfloat16
ROWS = 8
LANES = 128


def nearest_first(n):
    return sorted(range(1, n), key=lambda d: (min(d, n - d), d))


def farthest_first(n):
    return sorted(range(1, n), key=lambda d: (-min(d, n - d), d))


def self_product(rows):
    return lax.dot_general(rows, rows, (((0,), (0,)), ((), ())), preferred_element_type=F32)


def split(x, rows):
    return [x[k * rows : (k + 1) * rows] for k in range(x.shape[0] // rows)]


def columns_first(x):
    return jnp.concatenate([x] * (LANES // x.shape[0]), axis=0).T


def exchange_kernel(
    nu, ni, nt,
    coords_hbm, count_hbm, blocks, factor_hbm, item_hbm, hour_hbm,
    before_out, scaled_out, level_out,
    coords, count, factor, items, hours, tiles, terms, totals, from_core, from_x, mine_x, from_y,
    grams, g_core, g_y, g_sum, g_x, g_mine, g_other, gram,
    in_sem, tile_sem, z_send, z_recv, zh_send, zh_recv, y_send, y_recv, c_send, c_recv, x_send, x_recv,
    gc_send, gc_recv, gx_send, gx_recv, gy_send, gy_recv, go_send, go_recv, ga_send, ga_recv,
    rc_send, rc_recv, rx_send, rx_recv, ry_send, ry_recv,
):
    ny = nt // 2
    u = lax.axis_index("user")
    i = lax.axis_index("item")
    t = lax.axis_index("tm")
    y, c = t // 2, t % 2
    slots, width, _ = tiles.shape
    ri, rh = item_hbm.shape[0], hour_hbm.shape[0]
    share, rank = factor.shape
    strip_rows = rank // ny

    def at_user(d):
        return {"user": (u + d) % nu}

    def at_item(d):
        return {"item": (i + d) % ni}

    def at_y(d):
        return {"tm": ((y + d) % ny) * 2 + c}

    sibling = {"tm": y * 2 + 1 - c}

    def remote(src, dst, send, recv, device):
        return pltpu.make_async_remote_copy(
            src_ref=src, dst_ref=dst, send_sem=send, recv_sem=recv,
            device_id=device, device_id_type=pl.DeviceIdType.MESH,
        )

    def tile_copy(s):
        return pltpu.make_async_copy(blocks.at[s], tiles.at[s], tile_sem.at[s])

    own_rows = [
        pltpu.make_async_copy(item_hbm, items.at[t, u], z_recv.at[u]),
        pltpu.make_async_copy(hour_hbm, hours.at[i, u], zh_recv.at[u]),
    ]
    later = [
        pltpu.make_async_copy(factor_hbm, factor, in_sem.at[0]),
        pltpu.make_async_copy(coords_hbm, coords, in_sem.at[1]),
        pltpu.make_async_copy(count_hbm, count, in_sem.at[2]),
    ]

    barrier = pltpu.get_barrier_semaphore()
    partners = (
        [at_user(d) for d in farthest_first(nu)]
        + [at_item(d) for d in farthest_first(ni)]
        + [at_y(d) for d in farthest_first(ny)]
        + [sibling]
    )
    for device in partners:
        pl.semaphore_signal(barrier, inc=1, device_id=device, device_id_type=pl.DeviceIdType.MESH)
    for copy in own_rows:
        copy.start()
    pl.semaphore_wait(barrier, len(partners))

    sent = []

    def start(copy):
        copy.start()
        sent.append(copy)
        return copy

    for d in farthest_first(nu):
        start(remote(item_hbm, items.at[t, u], z_send.at[d], z_recv.at[u], at_user(d)))
    for d in farthest_first(nu):
        start(remote(hour_hbm, hours.at[i, u], zh_send.at[d], zh_recv.at[u], at_user(d)))
    for copy in later:
        copy.start()
    for s in range(slots):
        tile_copy(s).start()

    def wait_rows(rows, ref, send, recv):
        for v in range(nu)[rows]:
            remote(ref.at[v], ref.at[v], send.at[0], recv.at[v], at_user(1)).wait_recv()

    halves = [slice(0, nu // 2), slice(nu // 2, nu)]
    y_copies, c_copies = [{}, {}], []
    for k, half in enumerate(halves):
        wait_rows(half, items.at[t], z_send, z_recv)
        part = items.at[t, half]
        for d in farthest_first(ny):
            y_copies[k][d] = start(remote(part, part, y_send.at[k, d], y_recv.at[k, d], at_y(d)))
        c_copies.append(start(remote(part, part, c_send.at[k, 0], c_recv.at[k, 0], sibling)))
    wait_rows(slice(0, nu), hours.at[i], zh_send, zh_recv)
    x_copies = []
    for d in farthest_first(ni):
        x_copies.append(start(remote(hours.at[i], hours.at[i], x_send.at[d], x_recv.at[d], at_item(d))))

    def strip(v):
        return pl.ds(pl.multiple_of(v * strip_rows, strip_rows), strip_rows)

    grams[0] = self_product(hours[i].reshape(nu * rh, rank))
    grams[1] = self_product(items[t].reshape(nu * ri, rank))
    gc_copy = start(remote(grams.at[1 - c], g_core, gc_send, gc_recv, sibling))
    gc_copy.wait_recv()
    grams[c] = grams[c] + g_core[...]
    gy_copies = [
        start(remote(grams.at[c, strip((y + d) % ny)], g_y.at[d], gy_send.at[d], gy_recv.at[d], at_y(d)))
        for d in farthest_first(ny)
    ]

    for k, half in enumerate(halves):
        for d in nearest_first(ny):
            y_copies[k][d].wait_recv()
            part = items.at[((y + ny - d) % ny) * 2 + c, half]
            c_copies.append(start(remote(part, part, c_send.at[k, d], c_recv.at[k, d], sibling)))
    for copy in later:
        copy.wait()
    for copy in x_copies:
        copy.wait_recv()
    for copy in c_copies:
        copy.wait_recv()

    user_blocks = (share * ni * nt) // width
    item_blocks = (ri * nu * nt) // width
    hour_blocks = (rh * nu * ni) // width
    span = width // ri
    per_user = nt // span
    group = 16

    def product(s):
        tile_copy(s).wait()
        item_block = lax.rem(coords[1, 0, s], item_blocks)
        hour_block = lax.rem(coords[2, 0, s], hour_blocks)
        item_rows = (
            items[pl.ds(lax.rem(item_block, per_user) * span, span), lax.div(item_block, per_user)]
            .astype(F32)
            .reshape(width, rank)
        )
        hour_rows = hours[:, hour_block].astype(F32).reshape(width, rank)
        term = jnp.zeros((width, rank), F32)
        for g in range(width // group):
            khatri = jnp.concatenate(
                [(item_rows[j : j + 1, :] * hour_rows).astype(BF16) for j in range(g * group, (g + 1) * group)],
                axis=0,
            )
            part = tiles[s, :, g * group * width : (g + 1) * group * width]
            term = term + jnp.dot(part, khatri, preferred_element_type=F32)
        terms[s] = term

    pl.loop(0, slots // 2)(product)
    for copy in gy_copies:
        copy.wait_recv()
    g_total = grams[c, strip(y)]
    for d in range(1, ny):
        g_total = g_total + g_y[d]
    g_sum[...] = g_total
    gx_copies = [
        start(remote(g_sum, g_x.at[d], gx_send.at[d], gx_recv.at[d], at_item(d)))
        for d in farthest_first(ni)
    ]
    pl.loop(slots // 2, slots)(product)

    chunks = width // share
    reach = ny // 4
    near = 2 * reach + 1

    @pl.loop(0, user_blocks)
    def _(b):
        total = jnp.zeros((width, rank), F32)
        for s in range(slots):
            block = jnp.where(s < count[0, 0, 0], lax.rem(coords[0, 0, s], user_blocks), -1)
            hit = jnp.full((width, rank), block, jnp.int32) == b
            total = total + jnp.where(hit, terms[s], 0.0)
        for q in range(chunks):
            chip = b * (chunks // 2) + q // 2
            place = (chip % ny + ny - y + reach) % ny
            totals[q % 2, chip // ny, place] = total[q * share : (q + 1) * share]

    parts = [pl.ds(near, ny - near), pl.ds(0, near)]
    rc_copies = [
        start(
            remote(
                totals.at[1 - c, :, part], from_core.at[:, part], rc_send.at[k], rc_recv.at[k], sibling
            )
        )
        for k, part in enumerate(parts)
    ]
    rx_copies = [[], []]
    for k, part in enumerate(parts):
        rc_copies[k].wait_recv()
        totals[c, :, part] = totals[c, :, part] + from_core[:, part]
        for d in farthest_first(ni):
            rx_copies[k].append(
                start(
                    remote(
                        totals.at[c, (i + d) % ni, part], from_x.at[d, part],
                        rx_send.at[k, d], rx_recv.at[k, d], at_item(d),
                    )
                )
            )
    for copy in gx_copies:
        copy.wait_recv()
    g_total = g_sum[...]
    for d in range(1, ni):
        g_total = g_total + g_x[d]
    g_mine[...] = g_total
    go_copy = start(remote(g_mine, g_other, go_send, go_recv, sibling))
    go_copy.wait_recv()
    gram[strip(y), :] = g_mine[...] * g_other[...]
    ga_copies = [
        start(remote(gram.at[strip(y)], gram.at[strip(y)], ga_send.at[d], ga_recv.at[d], at_y(d)))
        for d in farthest_first(ny)
    ]

    ry_copies = []
    for k, part in enumerate(parts):
        for copy in rx_copies[k]:
            copy.wait_recv()
        summed = totals[c, i, part]
        for d in range(1, ni):
            summed = summed + from_x[d, part]
        mine_x[part] = summed
        for d in farthest_first(ny):
            place = (d + reach) % ny
            if (place >= near) == (k == 0):
                ry_copies.append(
                    start(remote(mine_x.at[place], from_y.at[d], ry_send.at[d], ry_recv.at[d], at_y(d)))
                )

    for copy in ga_copies:
        copy.wait_recv()
    weights = gram[...]
    current = factor[...]
    fitted = jnp.dot(current, weights, precision=lax.Precision.HIGHEST, preferred_element_type=F32)
    rows = lax.broadcasted_iota(jnp.int32, (rank, rank), 0)
    cols = lax.broadcasted_iota(jnp.int32, (rank, rank), 1)
    pivot = jnp.sum(jnp.where(rows == cols, weights, 0.0), axis=1, keepdims=True)
    pivot = jnp.broadcast_to(pivot, (rank, LANES))
    scaled = weights / pivot
    before = columns_first(current)

    for copy in ry_copies:
        copy.wait_recv()
    mttkrp = mine_x[reach]
    for d in range(1, ny):
        mttkrp = mttkrp + from_y[d]

    before_out[...] = before
    scaled_out[...] = scaled
    level_out[...] = before + columns_first(mttkrp - fitted) / pivot
    for copy in sent:
        copy.wait_send()


def sweep_kernel(before_ref, scaled_ref, level_ref, out):
    rank, share = level_ref.shape[0], out.shape[0]
    before, scaled, level = before_ref[...], scaled_ref[...], level_ref[...]
    place = lax.broadcasted_iota(jnp.int32, (ROWS, LANES), 0)
    fresh = []
    for g in range(rank // ROWS):
        low, high = g * ROWS, (g + 1) * ROWS
        head, rest = level[:ROWS], level[ROWS:]
        old = before[low:high]
        done = head
        for k in range(ROWS):
            new = jnp.maximum(head, 0.0)
            change = jnp.broadcast_to((new - old)[k : k + 1], (ROWS, LANES))
            done = jnp.where(place == k, new, done)
            if k < ROWS - 1:
                head = head - jnp.broadcast_to(scaled[low:high, low + k : low + k + 1], (ROWS, LANES)) * change
            if rest.shape[0]:
                full = jnp.concatenate([change] * (rest.shape[0] // ROWS), axis=0)
                rest = rest - jnp.broadcast_to(scaled[high:, low + k : low + k + 1], rest.shape) * full
        fresh.append(done)
        level = rest
    out[...] = jnp.concatenate(fresh, axis=0).T[:share]


def per_device(nu, ni, nt, blocks, block_coords, block_count, a_factor, item_factor, hour_factor):
    tiles = blocks.reshape(blocks.shape[3:])
    slots, width, depth = tiles.shape
    coords = jnp.transpose(block_coords, (0, 1, 4, 2, 3)).reshape(3, 1, slots)
    count = block_count.reshape((1, 1, 1))
    share, rank = a_factor.shape
    ri, rh = item_factor.shape[0], hour_factor.shape[0]
    ny = nt // 2
    strip_rows = rank // ny
    hbm = pl.BlockSpec(memory_space=pltpu.MemorySpace.HBM)
    on_chip = pl.BlockSpec(memory_space=pltpu.VMEM)
    vmem, smem, dma = pltpu.VMEM, pltpu.SMEM, pltpu.SemaphoreType.DMA
    ready = pl.pallas_call(
        functools.partial(exchange_kernel, nu, ni, nt),
        out_shape=(vmem((rank, LANES), F32), vmem((rank, rank), F32), vmem((rank, LANES), F32)),
        in_specs=[hbm] * 6,
        out_specs=[on_chip] * 3,
        scratch_shapes=[
            smem((3, 1, slots), jnp.int32),
            smem((1, 1, 1), jnp.int32),
            vmem((share, rank), F32),
            vmem((nt, nu, ri, rank), BF16),
            vmem((ni, nu, rh, rank), BF16),
            vmem((slots, width, depth), BF16),
            vmem((slots, width, rank), F32),
            vmem((2, ni, ny, share, rank), F32),
            vmem((ni, ny, share, rank), F32),
            vmem((ni, ny, share, rank), F32),
            vmem((ny, share, rank), F32),
            vmem((ny, share, rank), F32),
            vmem((2, rank, rank), F32),
            vmem((rank, rank), F32),
            vmem((ny, strip_rows, rank), F32),
            vmem((strip_rows, rank), F32),
            vmem((ni, strip_rows, rank), F32),
            vmem((strip_rows, rank), F32),
            vmem((strip_rows, rank), F32),
            vmem((rank, rank), F32),
            dma((3,)),
            dma((slots,)),
            dma((nu,)), dma((nu,)), dma((nu,)), dma((nu,)),
            dma((2, ny)), dma((2, ny)), dma((2, ny)), dma((2, ny)), dma((ni,)), dma((ni,)),
            dma, dma, dma((ni,)), dma((ni,)), dma((ny,)), dma((ny,)), dma, dma, dma((ny,)), dma((ny,)),
            dma((2,)), dma((2,)), dma((2, ni)), dma((2, ni)), dma((ny,)), dma((ny,)),
        ],
        compiler_params=pltpu.CompilerParams(
            collective_id=0, has_side_effects=True, vmem_limit_bytes=58 * 1024 * 1024
        ),
        name="exchange",
    )(coords, count, tiles, a_factor, item_factor, hour_factor)
    return pl.pallas_call(
        sweep_kernel,
        out_shape=jax.ShapeDtypeStruct((share, rank), F32),
        in_specs=[on_chip] * 3,
        out_specs=on_chip,
        compiler_params=pltpu.CompilerParams(vmem_limit_bytes=8 * 1024 * 1024),
        name="sweep",
    )(*ready)


def solution(mesh):
    placed = (
        P("user", "item", "tm", None, None, None),
        P("user", "item", "tm", None, None),
        P("user", "item", "tm"),
        P(("user", "item", "tm"), None),
        P(("item", "user", "tm"), None),
        P(("tm", "user", "item"), None),
    )
    return jax.shard_map(
        functools.partial(per_device, mesh.shape["user"], mesh.shape["item"], mesh.shape["tm"]),
        mesh=mesh,
        in_specs=placed,
        out_specs=P(("user", "item", "tm"), None),
        check_vma=False,
    )
```

time: 43.3 us -> 41.8 us (0.965)
  the two profiles are of different devices: /device:TPU:1 before, /device:TPU:8 now
where the time goes in v3:
time: 41.8 us; the launch traced here: 41.7 us
  Pallas kernels  41 us (98%)
  between operations  0.66 us (2%)
    pallas_call x1, Pallas kernels, per_device(): pl.pallas_call(functools.partial(exchange_kernel, nu, ni, nt), out_shape=...  39 us
    pallas_call x1, Pallas kernels, per_device(): pl.pallas_call(sweep_kernel, out_shape=jax.ShapeDtypeStruct((share, rank)...  2.07 us

profile of v3, /device:TPU:8, one launch (start us, length us, event | category | flops | bytes accessed | tf_op | source)
XLA Modules:
  0.0 41.7 jit_solution(271580454912025247)
XLA Ops:
  0.7 39.0 %exchange.1 = (f32[128,128]{1,0:T(8,128)S(1)}, f32[128,128]{1,0:T(8,128)S(1)}, f32[128,128]{1,0:T(8,128)S(1)}) custom-call(s32[3,1,8]{2,1,0:T(1,128)} %bitcast.5, s32[1,1,1]{2,1,0:T(1,128)S(6)} %copy.7.count_hbm, bf16[8,64,4096]{2,1,0:T(8,128)(2,1)} %bitcast.4, f32[16,128]{1,0:T(8,128)} %factor_hbm.1, bf16[8,128]{1,0:T(8,128)(2,1)} %item_hbm.1, ...), custom_call_target="tpu_custom_call" | custom-call | tf_op jit(solution)/shard_map/exchange/pallas_call | solution.py:325
  39.6 2.1 %sweep.1 = f32[16,128]{1,0:T(8,128)} custom-call(f32[128,128]{1,0:T(8,128)S(1)} %get-tuple-element.8.before_ref, f32[128,128]{1,0:T(8,128)S(1)} %get-tuple-element.9.scaled_ref, f32[128,128]{1,0:T(8,128)S(1)} %get-tuple-element.10.level_ref), custom_call_target="tpu_custom_call" | custom-call | tf_op jit(solution)/shard_map/sweep/pallas_call | solution.py:363

commit v4 on v3

--- a/solution.py
+++ b/solution.py
@@ -29,6 +29,15 @@
     return [x[k * rows : (k + 1) * rows] for k in range(x.shape[0] // rows)]
 
 
+def column_places(rank):
+    places, start = [], 0
+    for r in range(rank):
+        first_row = r // ROWS * ROWS
+        places.append((first_row, start))
+        start += rank - first_row
+    return places
+
+
 def columns_first(x):
     return jnp.concatenate([x] * (LANES // x.shape[0]), axis=0).T
 
@@ -36,10 +45,10 @@
 def exchange_kernel(
     nu, ni, nt,
     coords_hbm, count_hbm, blocks, factor_hbm, item_hbm, hour_hbm,
-    before_out, scaled_out, level_out,
-    coords, count, factor, items, hours, tiles, terms, totals, from_core, from_x, mine_x, from_y,
+    wide_out, level_out,
+    coords, count, factor, rows_u, items, hours, tiles, terms, totals, from_core, from_x, mine_x, from_y,
     grams, g_core, g_y, g_sum, g_x, g_mine, g_other, gram,
-    in_sem, tile_sem, z_send, z_recv, zh_send, zh_recv, y_send, y_recv, c_send, c_recv, x_send, x_recv,
+    in_sem, tile_sem, z_send, z_recv, y_send, y_recv, c_send, c_recv, x_send, x_recv,
     gc_send, gc_recv, gx_send, gx_recv, gy_send, gy_recv, go_send, go_recv, ga_send, ga_recv,
     rc_send, rc_recv, rx_send, rx_recv, ry_send, ry_recv,
 ):
@@ -52,6 +61,9 @@
     ri, rh = item_hbm.shape[0], hour_hbm.shape[0]
     share, rank = factor.shape
     strip_rows = rank // ny
+    pieces = rh // ri
+    reach = ny // 4
+    near = 2 * reach + 1
 
     def at_user(d):
         return {"user": (u + d) % nu}
@@ -62,7 +74,10 @@
     def at_y(d):
         return {"tm": ((y + d) % ny) * 2 + c}
 
-    sibling = {"tm": y * 2 + 1 - c}
+    def at_other(d):
+        return {"tm": ((y + d) % ny) * 2 + 1 - c}
+
+    sibling = at_other(0)
 
     def remote(src, dst, send, recv, device):
         return pltpu.make_async_remote_copy(
@@ -73,15 +88,18 @@
     def tile_copy(s):
         return pltpu.make_async_copy(blocks.at[s], tiles.at[s], tile_sem.at[s])
 
-    own_rows = [
-        pltpu.make_async_copy(item_hbm, items.at[t, u], z_recv.at[u]),
-        pltpu.make_async_copy(hour_hbm, hours.at[i, u], zh_recv.at[u]),
+    own_rows = [pltpu.make_async_copy(item_hbm, rows_u.at[u, 0], in_sem.at[3])] + [
+        pltpu.make_async_copy(hour_hbm.at[q * ri : (q + 1) * ri], rows_u.at[u, 1 + q], in_sem.at[4 + q])
+        for q in range(pieces)
     ]
     later = [
         pltpu.make_async_copy(factor_hbm, factor, in_sem.at[0]),
         pltpu.make_async_copy(coords_hbm, coords, in_sem.at[1]),
         pltpu.make_async_copy(count_hbm, count, in_sem.at[2]),
     ]
+
+    for copy in own_rows:
+        copy.start()
 
     barrier = pltpu.get_barrier_semaphore()
     partners = (
@@ -92,10 +110,10 @@
     )
     for device in partners:
         pl.semaphore_signal(barrier, inc=1, device_id=device, device_id_type=pl.DeviceIdType.MESH)
+    pl.semaphore_wait(barrier, len(partners))
+
     for copy in own_rows:
-        copy.start()
-    pl.semaphore_wait(barrier, len(partners))
-
+        copy.wait()
     sent = []
 
     def start(copy):
@@ -104,36 +122,30 @@
         return copy
 
     for d in farthest_first(nu):
-        start(remote(item_hbm, items.at[t, u], z_send.at[d], z_recv.at[u], at_user(d)))
-    for d in farthest_first(nu):
-        start(remote(hour_hbm, hours.at[i, u], zh_send.at[d], zh_recv.at[u], at_user(d)))
+        start(remote(rows_u.at[u], rows_u.at[u], z_send.at[d], z_recv.at[u], at_user(d)))
     for copy in later:
         copy.start()
     for s in range(slots):
         tile_copy(s).start()
-
-    def wait_rows(rows, ref, send, recv):
-        for v in range(nu)[rows]:
-            remote(ref.at[v], ref.at[v], send.at[0], recv.at[v], at_user(1)).wait_recv()
-
-    halves = [slice(0, nu // 2), slice(nu // 2, nu)]
-    y_copies, c_copies = [{}, {}], []
-    for k, half in enumerate(halves):
-        wait_rows(half, items.at[t], z_send, z_recv)
-        part = items.at[t, half]
-        for d in farthest_first(ny):
-            y_copies[k][d] = start(remote(part, part, y_send.at[k, d], y_recv.at[k, d], at_y(d)))
-        c_copies.append(start(remote(part, part, c_send.at[k, 0], c_recv.at[k, 0], sibling)))
-    wait_rows(slice(0, nu), hours.at[i], zh_send, zh_recv)
-    x_copies = []
-    for d in farthest_first(ni):
-        x_copies.append(start(remote(hours.at[i], hours.at[i], x_send.at[d], x_recv.at[d], at_item(d))))
+    for v in range(nu):
+        pl.when(u != v)(remote(rows_u.at[v], rows_u.at[v], z_send.at[0], z_recv.at[v], at_user(1)).wait_recv)
+
+    own_items, own_hours = rows_u.at[:, 0], rows_u.at[:, pl.ds(1, pieces)]
+    y_copies = {
+        d: start(remote(own_items, items.at[c, (reach + ny - d) % ny], y_send.at[d], y_recv.at[d], at_y(d)))
+        for d in farthest_first(ny)
+    }
+    x_copies = [
+        start(remote(own_hours, hours.at[i], x_send.at[d], x_recv.at[d], at_item(d))) for d in farthest_first(ni)
+    ]
+    items[c, reach] = own_items[...]
+    hours[i] = own_hours[...]
 
     def strip(v):
         return pl.ds(pl.multiple_of(v * strip_rows, strip_rows), strip_rows)
 
-    grams[0] = self_product(hours[i].reshape(nu * rh, rank))
-    grams[1] = self_product(items[t].reshape(nu * ri, rank))
+    grams[0] = self_product(own_hours[...].reshape(nu * rh, rank))
+    grams[1] = self_product(own_items[...].reshape(nu * ri, rank))
     gc_copy = start(remote(grams.at[1 - c], g_core, gc_send, gc_recv, sibling))
     gc_copy.wait_recv()
     grams[c] = grams[c] + g_core[...]
@@ -142,11 +154,12 @@
         for d in farthest_first(ny)
     ]
 
-    for k, half in enumerate(halves):
+    c_copies = []
+    for k, part in enumerate([pl.ds(0, near), pl.ds(near, ny - near)]):
         for d in nearest_first(ny):
-            y_copies[k][d].wait_recv()
-            part = items.at[((y + ny - d) % ny) * 2 + c, half]
-            c_copies.append(start(remote(part, part, c_send.at[k, d], c_recv.at[k, d], sibling)))
+            if ((reach + ny - d) % ny >= near) == bool(k):
+                y_copies[d].wait_recv()
+        c_copies.append(start(remote(items.at[c, part], items.at[c, part], c_send.at[k], c_recv.at[k], sibling)))
     for copy in later:
         copy.wait()
     for copy in x_copies:
@@ -165,11 +178,12 @@
         tile_copy(s).wait()
         item_block = lax.rem(coords[1, 0, s], item_blocks)
         hour_block = lax.rem(coords[2, 0, s], hour_blocks)
-        item_rows = (
-            items[pl.ds(lax.rem(item_block, per_user) * span, span), lax.div(item_block, per_user)]
-            .astype(F32)
-            .reshape(width, rank)
-        )
+        chip = lax.div(lax.rem(item_block, per_user) * span, 2) + ny - y + reach
+        owner = lax.div(item_block, per_user)
+        item_rows = [
+            items[core, lax.rem(chip + step, ny), owner] for step in range(span // 2) for core in range(2)
+        ]
+        item_rows = jnp.concatenate([rows.astype(F32) for rows in item_rows], axis=0)
         hour_rows = hours[:, hour_block].astype(F32).reshape(width, rank)
         term = jnp.zeros((width, rank), F32)
         for g in range(width // group):
@@ -195,8 +209,6 @@
     pl.loop(slots // 2, slots)(product)
 
     chunks = width // share
-    reach = ny // 4
-    near = 2 * reach + 1
 
     @pl.loop(0, user_blocks)
     def _(b):
@@ -265,13 +277,19 @@
         copy.wait_recv()
     weights = gram[...]
     current = factor[...]
-    fitted = jnp.dot(current, weights, precision=lax.Precision.HIGHEST, preferred_element_type=F32)
     rows = lax.broadcasted_iota(jnp.int32, (rank, rank), 0)
     cols = lax.broadcasted_iota(jnp.int32, (rank, rank), 1)
+    fitted = jnp.dot(
+        current, jnp.where(rows > cols, weights, 0.0), precision=lax.Precision.HIGHEST, preferred_element_type=F32
+    )
     pivot = jnp.sum(jnp.where(rows == cols, weights, 0.0), axis=1, keepdims=True)
     pivot = jnp.broadcast_to(pivot, (rank, LANES))
     scaled = weights / pivot
-    before = columns_first(current)
+    for r, (first_row, start_row) in enumerate(column_places(rank)):
+        rows_below = rank - first_row
+        wide_out[start_row : start_row + rows_below] = jnp.broadcast_to(
+            scaled[first_row:, r : r + 1], (rows_below, LANES)
+        )
 
     for copy in ry_copies:
         copy.wait_recv()
@@ -279,32 +297,29 @@
     for d in range(1, ny):
         mttkrp = mttkrp + from_y[d]
 
-    before_out[...] = before
-    scaled_out[...] = scaled
-    level_out[...] = before + columns_first(mttkrp - fitted) / pivot
+    level_out[...] = columns_first(mttkrp - fitted) / pivot
     for copy in sent:
         copy.wait_send()
 
 
-def sweep_kernel(before_ref, scaled_ref, level_ref, out):
+def sweep_kernel(wide, level_ref, out):
     rank, share = level_ref.shape[0], out.shape[0]
-    before, scaled, level = before_ref[...], scaled_ref[...], level_ref[...]
+    level = level_ref[...]
     place = lax.broadcasted_iota(jnp.int32, (ROWS, LANES), 0)
     fresh = []
-    for g in range(rank // ROWS):
-        low, high = g * ROWS, (g + 1) * ROWS
+    for first_row in range(0, rank, ROWS):
         head, rest = level[:ROWS], level[ROWS:]
-        old = before[low:high]
         done = head
         for k in range(ROWS):
+            row = column_places(rank)[first_row + k][1]
             new = jnp.maximum(head, 0.0)
-            change = jnp.broadcast_to((new - old)[k : k + 1], (ROWS, LANES))
             done = jnp.where(place == k, new, done)
+            column = jnp.broadcast_to(new[k : k + 1], (ROWS, LANES))
             if k < ROWS - 1:
-                head = head - jnp.broadcast_to(scaled[low:high, low + k : low + k + 1], (ROWS, LANES)) * change
+                head = head - wide[row : row + ROWS] * column
             if rest.shape[0]:
-                full = jnp.concatenate([change] * (rest.shape[0] // ROWS), axis=0)
-                rest = rest - jnp.broadcast_to(scaled[high:, low + k : low + k + 1], rest.shape) * full
+                full = jnp.concatenate([column] * (rest.shape[0] // ROWS), axis=0)
+                rest = rest - wide[row + ROWS : row + ROWS + rest.shape[0]] * full
         fresh.append(done)
         level = rest
     out[...] = jnp.concatenate(fresh, axis=0).T[:share]
@@ -319,20 +334,23 @@
     ri, rh = item_factor.shape[0], hour_factor.shape[0]
     ny = nt // 2
     strip_rows = rank // ny
+    pieces = rh // ri
+    wide_rows = sum(rank - first_row for first_row, _ in column_places(rank))
     hbm = pl.BlockSpec(memory_space=pltpu.MemorySpace.HBM)
     on_chip = pl.BlockSpec(memory_space=pltpu.VMEM)
     vmem, smem, dma = pltpu.VMEM, pltpu.SMEM, pltpu.SemaphoreType.DMA
     ready = pl.pallas_call(
         functools.partial(exchange_kernel, nu, ni, nt),
-        out_shape=(vmem((rank, LANES), F32), vmem((rank, rank), F32), vmem((rank, LANES), F32)),
+        out_shape=(vmem((wide_rows, LANES), F32), vmem((rank, LANES), F32)),
         in_specs=[hbm] * 6,
-        out_specs=[on_chip] * 3,
+        out_specs=[on_chip] * 2,
         scratch_shapes=[
             smem((3, 1, slots), jnp.int32),
             smem((1, 1, 1), jnp.int32),
             vmem((share, rank), F32),
-            vmem((nt, nu, ri, rank), BF16),
-            vmem((ni, nu, rh, rank), BF16),
+            vmem((nu, 1 + pieces, ri, rank), BF16),
+            vmem((2, ny, nu, ri, rank), BF16),
+            vmem((ni, nu, pieces, ri, rank), BF16),
             vmem((slots, width, depth), BF16),
             vmem((slots, width, rank), F32),
             vmem((2, ni, ny, share, rank), F32),
@@ -348,22 +366,22 @@
             vmem((strip_rows, rank), F32),
             vmem((strip_rows, rank), F32),
             vmem((rank, rank), F32),
-            dma((3,)),
+            dma((4 + pieces,)),
             dma((slots,)),
-            dma((nu,)), dma((nu,)), dma((nu,)), dma((nu,)),
-            dma((2, ny)), dma((2, ny)), dma((2, ny)), dma((2, ny)), dma((ni,)), dma((ni,)),
+            dma((nu,)), dma((nu,)),
+            dma((ny,)), dma((ny,)), dma((2,)), dma((2,)), dma((ni,)), dma((ni,)),
             dma, dma, dma((ni,)), dma((ni,)), dma((ny,)), dma((ny,)), dma, dma, dma((ny,)), dma((ny,)),
             dma((2,)), dma((2,)), dma((2, ni)), dma((2, ni)), dma((ny,)), dma((ny,)),
         ],
         compiler_params=pltpu.CompilerParams(
-            collective_id=0, has_side_effects=True, vmem_limit_bytes=58 * 1024 * 1024
+            collective_id=0, has_side_effects=True, vmem_limit_bytes=54 * 1024 * 1024
         ),
         name="exchange",
     )(coords, count, tiles, a_factor, item_factor, hour_factor)
     return pl.pallas_call(
         sweep_kernel,
         out_shape=jax.ShapeDtypeStruct((share, rank), F32),
-        in_specs=[on_chip] * 3,
+        in_specs=[on_chip] * 2,
         out_specs=on_chip,
         compiler_params=pltpu.CompilerParams(vmem_limit_bytes=8 * 1024 * 1024),
         name="sweep",

time: 41.8 us -> 40.9 us (0.978)
  the two profiles are of different devices: /device:TPU:8 before, /device:TPU:1 now
where the time goes in v4:
time: 40.9 us; the launch traced here: 40.3 us
  Pallas kernels  39.6 us (97%)
  between operations  0.66 us (2%)
    pallas_call x1, Pallas kernels, per_device(): pl.pallas_call(functools.partial(exchange_kernel, nu, ni, nt), out_shape=...  38.4 us
    pallas_call x1, Pallas kernels, per_device(): pl.pallas_call(sweep_kernel, out_shape=jax.ShapeDtypeStruct((share, rank)...  1.24 us

profile of v4, /device:TPU:1, one launch (start us, length us, event | category | flops | bytes accessed | tf_op | source)
XLA Modules:
  0.0 40.3 jit_solution(3894759872862873006)
XLA Ops:
  0.7 38.4 %exchange.1 = (f32[8704,128]{1,0:T(8,128)S(1)}, f32[128,128]{1,0:T(8,128)S(1)}) custom-call(s32[3,1,8]{2,1,0:T(1,128)} %bitcast.5, s32[1,1,1]{2,1,0:T(1,128)S(6)} %copy.7.count_hbm, bf16[8,64,4096]{2,1,0:T(8,128)(2,1)} %bitcast.4, f32[16,128]{1,0:T(8,128)} %factor_hbm.1, bf16[8,128]{1,0:T(8,128)(2,1)} %item_hbm.1, bf16[16,128]{1,0:T(8,128)(2,1)} %hour_hbm.1), custom_call_target="tpu_custom_call" | custom-call | tf_op jit(solution)/shard_map/exchange/pallas_call | solution.py:342
  39.0 1.2 %sweep.1 = f32[16,128]{1,0:T(8,128)} custom-call(f32[8704,128]{1,0:T(8,128)S(1)} %get-tuple-element.7.wide, f32[128,128]{1,0:T(8,128)S(1)} %get-tuple-element.8.level_ref), custom_call_target="tpu_custom_call" | custom-call | tf_op jit(solution)/shard_map/sweep/pallas_call | solution.py:381

commit v5 on v4

--- a/solution.py
+++ b/solution.py
@@ -258,7 +258,7 @@
         for d in farthest_first(ny)
     ]
 
-    ry_copies = []
+    ry_copies = {}
     for k, part in enumerate(parts):
         for copy in rx_copies[k]:
             copy.wait_recv()
@@ -269,8 +269,8 @@
         for d in farthest_first(ny):
             place = (d + reach) % ny
             if (place >= near) == (k == 0):
-                ry_copies.append(
-                    start(remote(mine_x.at[place], from_y.at[d], ry_send.at[d], ry_recv.at[d], at_y(d)))
+                ry_copies[d] = start(
+                    remote(mine_x.at[place], from_y.at[d], ry_send.at[d], ry_recv.at[d], at_y(d))
                 )
 
     for copy in ga_copies:
@@ -291,10 +291,9 @@
             scaled[first_row:, r : r + 1], (rows_below, LANES)
         )
 
-    for copy in ry_copies:
-        copy.wait_recv()
     mttkrp = mine_x[reach]
-    for d in range(1, ny):
+    for d in nearest_first(ny):
+        ry_copies[d].wait_recv()
         mttkrp = mttkrp + from_y[d]
 
     level_out[...] = columns_first(mttkrp - fitted) / pivot

time: 40.9 us -> 40.9 us (level)
  no operation moved by 1% of the time
where the time goes in v5:
time: 40.9 us; the launch traced here: 40.2 us
  Pallas kernels  39.6 us (97%)
  between operations  0.66 us (2%)
    pallas_call x1, Pallas kernels, per_device(): pl.pallas_call(functools.partial(exchange_kernel, nu, ni, nt), out_shape=...  38.3 us
    pallas_call x1, Pallas kernels, per_device(): pl.pallas_call(sweep_kernel, out_shape=jax.ShapeDtypeStruct((share, rank)...  1.24 us

profile of v5, /device:TPU:1, one launch (start us, length us, event | category | flops | bytes accessed | tf_op | source)
XLA Modules:
  0.0 40.2 jit_solution(14144347137643503691)
XLA Ops:
  0.7 38.3 %exchange.1 = (f32[8704,128]{1,0:T(8,128)S(1)}, f32[128,128]{1,0:T(8,128)S(1)}) custom-call(s32[3,1,8]{2,1,0:T(1,128)} %bitcast.5, s32[1,1,1]{2,1,0:T(1,128)S(6)} %copy.7.count_hbm, bf16[8,64,4096]{2,1,0:T(8,128)(2,1)} %bitcast.4, f32[16,128]{1,0:T(8,128)} %factor_hbm.1, bf16[8,128]{1,0:T(8,128)(2,1)} %item_hbm.1, bf16[16,128]{1,0:T(8,128)(2,1)} %hour_hbm.1), custom_call_target="tpu_custom_call" | custom-call | tf_op jit(solution)/shard_map/exchange/pallas_call | solution.py:341
  39.0 1.2 %sweep.1 = f32[16,128]{1,0:T(8,128)} custom-call(f32[8704,128]{1,0:T(8,128)S(1)} %get-tuple-element.7.wide, f32[128,128]{1,0:T(8,128)S(1)} %get-tuple-element.8.level_ref), custom_call_target="tpu_custom_call" | custom-call | tf_op jit(solution)/shard_map/sweep/pallas_call | solution.py:380
